TPU v7x, 32 devices: a whole 2x2x4 slice. The times are simulated.
32 devices in a mesh: groups: 2 (over y), frame: 8 (over z, x), row: 2 (over core).
Axes of the slice: x: 2, y: 2, z: 4, core: 2. Of those that a mesh axis runs over, the one named last changes fastest.
Arguments:
- latent: bfloat16 [16, 16, 64, 640], P(('groups', 'frame'), 'row'), parts along dimension 0, may hold values from -18 to 18
- norm_gain: float32 [640], replicated, may hold values from 0.1 to 1.9
- time_kernel: bfloat16 [3, 640, 640], replicated, may hold values from -0.125 to 0.125
- space_norm: float32 [640], replicated, may hold values from 0.1 to 1.9
- space_qkv: bfloat16 [640, 1920], replicated, may hold values from -12 to 12
- space_out: bfloat16 [640, 640], replicated, may hold values from -0.25 to 0.25
- time_norm: float32 [640], replicated, may hold values from 0.1 to 1.9
- time_qkv: bfloat16 [640, 1920], replicated, may hold values from -12 to 12
- time_out: bfloat16 [640, 640], replicated, may hold values from -0.25 to 0.25
Outputs:
- output: float32 [16, 16, 64, 640], P(('groups', 'frame'), 'row'), parts along dimension 0
There are 2 independent parts, one for each index of `groups`. A program takes and returns all parts, laid end to end along the dimension named above; an argument that names none is the same for every part. Nothing has to cross between parts.
All inputs are finite; a program needn't handle non-finite values.
Results may differ from a plain program's by a relative error of at most 0.0018.
Values may be sent and summed in bfloat16 or wider, within the bound.
A program may use at most 128 MiB of HBM per device.

v0:
```python
import jax
import jax.numpy as jnp
from jax import lax
from jax.sharding import PartitionSpec as P

HEADS = 10
GROUPS = 32
epsilon = 1e-05


def padded_2(block, sides, width):
    for axis, dim in sides:
        count = lax.axis_size(axis)
        forward = [(i, i + 1) for i in range(count - 1)]
        backward = [(target, source) for source, target in forward]
        low = lax.ppermute(
            lax.slice_in_dim(block, block.shape[dim] - width, None, axis=dim), axis, forward
        )
        high = lax.ppermute(lax.slice_in_dim(block, 0, width, axis=dim), axis, backward)
        block = jnp.concatenate([low, block, high], axis=dim)
    return block


def normalize_silu(grouped, first, second, number, gain, shape):
    center = first / number
    spread = second / number - center * center
    scaling = lax.rsqrt(spread + epsilon)
    normed = ((grouped - center[:, None]) * scaling[:, None]).reshape(shape) * gain
    return jax.nn.silu(normed).astype(jnp.bfloat16)


def layer_norm(inputs, gain):
    center = jnp.mean(inputs, axis=-1, keepdims=True)
    shifted = inputs - center
    spread = jnp.mean(shifted * shifted, axis=-1, keepdims=True)
    return (shifted * lax.rsqrt(spread + epsilon) * gain).astype(jnp.bfloat16)


def project_three(inputs, weight):
    channels = weight.shape[0]
    lead = inputs.shape[:-1]
    packed = jnp.dot(
        inputs.reshape(-1, channels), weight, preferred_element_type=jnp.float32
    ).astype(jnp.bfloat16)
    packed = packed.reshape(lead + (3 * channels,))
    return (
        packed[..., :channels],
        packed[..., channels : 2 * channels],
        packed[..., 2 * channels :],
    )


def time_attend(queries, key_rows, values):
    frames, pixels, channels = queries.shape
    head_size = channels // HEADS
    query_heads = queries.reshape(frames, pixels, HEADS, head_size)
    key_heads = key_rows.reshape(frames, pixels, HEADS, head_size)
    value_heads = values.reshape(frames, pixels, HEADS, head_size)
    scores = jnp.einsum(
        "qphd,kphd->phqk", query_heads, key_heads, preferred_element_type=jnp.float32
    ) * head_size ** (-0.5)
    raised = jnp.exp(scores - jnp.max(scores, axis=-1, keepdims=True))
    weight_sum = jnp.sum(raised, axis=-1)
    weights = raised.astype(jnp.bfloat16)
    result = jnp.einsum("phqk,kphd->qphd", weights, value_heads, preferred_element_type=jnp.float32)
    result = result / jnp.transpose(weight_sum, (2, 0, 1))[:, :, :, None]
    return result.astype(jnp.bfloat16).reshape(frames, pixels, channels)


def add_projected(base, attended, weight):
    channels = weight.shape[0]
    summed = base.reshape(-1, channels) + jnp.dot(
        attended.reshape(-1, channels), weight, preferred_element_type=jnp.float32
    )
    return summed.reshape(base.shape)


def body(
    latent, norm_gain, time_kernel, space_norm, space_qkv, space_out, time_norm, time_qkv, time_out
):
    frames, row_count, col_count, channels = latent.shape
    pixels = row_count * col_count
    per_group = channels // GROUPS
    head_size = channels // HEADS
    grouped = latent.astype(jnp.float32).reshape(frames, row_count, col_count, GROUPS, per_group)
    first = jnp.sum(grouped, axis=(0, 1, 2, 4))
    second = jnp.sum(grouped * grouped, axis=(0, 1, 2, 4))
    first, second = lax.psum((first, second), ("frame", "row"))
    number = frames * lax.axis_size("frame") * pixels * lax.axis_size("row") * per_group
    wide = padded_2(latent, (("frame", 0),), 1)
    wide_frames = wide.shape[0]
    wide_grouped = wide.astype(jnp.float32).reshape(
        wide_frames, row_count, col_count, GROUPS, per_group
    )
    padded = normalize_silu(wide_grouped, first, second, number, norm_gain, wide.shape)
    me, count = (lax.axis_index("frame"), lax.axis_size("frame"))
    place = me * frames - 1 + jnp.arange(wide_frames)
    inside = (place >= 0) & (place < count * frames)
    padded = jnp.where(inside[:, None, None, None], padded, jnp.zeros((), padded.dtype))
    mixed = jnp.zeros((frames * pixels, channels), jnp.float32)
    for tap in range(3):
        window = padded[tap : tap + frames].reshape(-1, channels)
        mixed = mixed + jnp.dot(window, time_kernel[tap], preferred_element_type=jnp.float32)
    stepped = latent.astype(jnp.float32).reshape(-1, channels) + mixed
    stepped = stepped.reshape(frames, pixels, channels)
    tokens = layer_norm(stepped, space_norm)
    queries, key_rows, values = project_three(tokens, space_qkv)
    query_heads = queries.reshape(frames, pixels, HEADS, head_size)
    top_score = jnp.full((frames, HEADS, pixels), -jnp.inf, jnp.float32)
    weight_sum = jnp.zeros((frames, HEADS, pixels), jnp.float32)
    partial_sum = jnp.zeros((frames, HEADS, pixels, head_size), jnp.float32)
    key_piece = lax.all_gather(key_rows, "row", axis=1, tiled=True)
    value_piece = lax.all_gather(values, "row", axis=1, tiled=True)
    key_count = key_piece.shape[1]
    key_heads = key_piece.reshape(frames, key_count, HEADS, head_size)
    value_heads = value_piece.reshape(frames, key_count, HEADS, head_size)
    scores = jnp.einsum(
        "fqhd,fkhd->fhqk", query_heads, key_heads, preferred_element_type=jnp.float32
    ) * head_size ** (-0.5)
    new_top = jnp.max(scores, axis=-1)
    rescale = jnp.exp(top_score - new_top)
    raised = jnp.exp(scores - new_top[..., None])
    weight_sum = weight_sum * rescale + jnp.sum(raised, axis=-1)
    weights = raised.astype(jnp.bfloat16)
    partial_sum = partial_sum * rescale[..., None] + jnp.einsum(
        "fhqk,fkhd->fhqd", weights, value_heads, preferred_element_type=jnp.float32
    )
    top_score, weight_sum, partial_sum = (new_top, weight_sum, partial_sum)
    attended = (partial_sum / weight_sum[..., None]).astype(jnp.bfloat16)
    attended = jnp.transpose(attended, (0, 2, 1, 3)).reshape(frames, pixels, channels)
    spaced = add_projected(stepped, attended, space_out)
    normed = layer_norm(spaced, time_norm)
    moved = lax.all_to_all(normed, "frame", split_axis=1, concat_axis=0, tiled=True)
    queries, key_rows, values = project_three(moved, time_qkv)
    result = time_attend(queries, key_rows, values)
    result = lax.all_to_all(result, "frame", split_axis=0, concat_axis=1, tiled=True)
    output = add_projected(spaced, result, time_out)
    return output.reshape(frames, row_count, col_count, channels)


def solution(mesh):
    return jax.shard_map(
        body,
        mesh=mesh,
        in_specs=(
            P(("groups", "frame"), "row", None, None),
            P(),
            P(),
            P(),
            P(),
            P(),
            P(),
            P(),
            P(),
        ),
        out_specs=P(("groups", "frame"), "row", None, None),
        check_vma=False,
    )
```

profile of v0, /device:TPU:0, one launch (start us, length us, event | category | flops | bytes accessed | tf_op | source)
XLA Modules:
  0.0 192.2 jit_solution(7589339824454949340)
XLA Ops:
  6.5 5.0 %collective-permute-start = (bf16[1,8,64,640]{3,2,1,0:T(8,128)(2,1)}, bf16[1,8,64,640]{3,2,1,0:T(8,128)(2,1)S(1)}, u32[]{:S(2)}, u32[]{:S(2)}) collective-permute-start(bf16[1,8,64,640]{3,2,1,0:T(8,128)(2,1)} %param.9), channel_id=1, source_target_pairs={{0,2},{2,4},{4,6},{6,8},{8,10},{10,12},{12,14},{1,3},{3,5},{5,7},{... | collective-permute-start | bytes 1966088 | tf_op jit(solution)/shard_map/ppermute | solution.py:16
  11.6 1.3 collective-permute-start.1
  12.9 1.3 convert_reduce_fusion
  14.2 0.1 reduce_sum.87
  14.3 0.1 reduce_sum.90
  14.4 0.1 reduce_sum.88
  14.5 0.1 reduce_sum.91
  14.6 49.5 %all-reduce = (f32[32]{0:T(128)S(1)}, f32[32]{0:T(128)S(1)}) all-reduce(f32[32]{0:T(128)S(1)} %reduce_sum.91, f32[32]{0:T(128)S(1)} %reduce_sum.88), channel_id=1, replica_groups=mesh['groups'=2,'frame'=8,'row'=2] {'frame','row'}, use_global_device_ids=true, to_apply=%region_5.6 | all-reduce | flops 64 | bytes 512 | tf_op jit(solution)/shard_map/psum | solution.py:88
  64.1 0.1 mul.98
  64.2 0.1 mul.99
  64.3 0.1 sub.68
  64.4 0.1 sub.69
  64.5 2.5 %fusion.8 = bf16[3,8,64,640]{3,2,1,0:T(8,128)(2,1)S(1)} fusion(bf16[1,8,64,640]{3,2,1,0:T(8,128)(2,1)} %collective-permute-done.1, bf16[1,8,64,640]{3,2,1,0:T(8,128)(2,1)} %param.9, bf16[1,8,64,640]{3,2,1,0:T(8,128)(2,1)S(1)} %collective-permute-done, f32[640]{0:T(1024)} %param.10, f32[640]{0:T(1024)S(1)} %mul.99, f32[640]{0:T(1024)S(1)} %sub.69, ...), kind=kLoop, calls=%fused_computation.15 | loop fusion | flops 11796480 | bytes 3939843 | tf_op jit(solution)/shard_map/jit(_where)/select_n | solution.py:99
  67.0 0.0 copy-start.7
  67.1 0.2 fusion.38
  67.3 1.5 copy-done.7
  68.7 0.7 fusion.19
  69.5 0.0 copy-start.6
  69.5 0.7 fusion.21
  70.3 0.3 copy-done.6
  70.6 0.9 fusion.39
  71.5 0.3 multiply_reduce_fusion.3
  71.9 1.9 fusion.4
  73.8 1.2 fusion.37
  75.0 0.0 all-gather.3.cloned.1.call-update
  75.0 0.2 all-gather.5.cloned.1.call-start
  75.2 0.3 copy.50
  75.5 0.3 all-gather.5.cloned.1.call-update
  75.8 6.1 %all-gather.3.cloned.1.call-done = bf16[1,1024,640]{2,1,0:T(8,128)(2,1)} async-done(((bf16[1,512,640]{2,1,0:T(8,128)(2,1)}), bf16[1,1024,640]{2,1,0:T(8,128)(2,1)}) %all-gather.3.cloned.1.call-update) | async-done | bytes 1310736 | tf_op jit(solution)/shard_map/all_gather | solution.py:112
  81.9 1.6 copy.51
  83.5 3.0 %multiply_reduce_fusion = (f32[10,512]{1,0:T(8,128)S(1)}, f32[10,512,1024]{2,1,0:T(8,128)S(1)}) fusion(bf16[512,10,64]{0,2,1:T(8,128)(2,1)S(1)} %bitcast.69, bf16[1024,10,64]{0,2,1:T(8,128)(2,1)S(1)} %bitcast.63), kind=kOutput, calls=%fused_computation.1 | convolution fusion | flops 681569280 | bytes 22958080 | tf_op jit(solution)/shard_map/fqhd,fkhd->fhqk/dot_general | solution.py:117
  86.5 4.6 %fusion = f32[10,512]{1,0:T(8,128)S(1)} fusion(f32[10,512,1024]{2,1,0:T(8,128)S(1)} %get-tuple-element.25, f32[10,512]{1,0:T(8,128)S(1)} %get-tuple-element.24), kind=kLoop, calls=%fused_computation.2 | loop fusion | flops 15723520 | bytes 21012480 | tf_op jit(solution)/shard_map/reduce_sum | solution.py:123
  91.1 3.0 %copy-done.2 = f32[10,512,1024]{2,1,0:T(8,128)} copy-done((f32[10,512,1024]{2,1,0:T(8,128)}, f32[10,512,1024]{2,1,0:T(8,128)S(1)}, u32[]{:S(2)}) %copy-start.2) | copy-done | bytes 20971544
  94.1 0.0 all-gather.5.cloned.1.call-done
  94.1 1.6 copy.52
  95.7 0.0 copy-start.5
  95.8 9.4 %divide_convert_fusion = bf16[10,512,64]{1,2,0:T(8,128)(2,1)S(1)} fusion(bf16[1024,10,64]{0,2,1:T(8,128)(2,1)S(1)} %bitcast.75, f32[10,512,1024]{2,1,0:T(8,128)} %copy-done.2, f32[10,512]{1,0:T(8,128)S(1)} %get-tuple-element.24, f32[10,512]{1,0:T(8,128)S(1)} %get-tuple-element.19, f32[10,512]{1,0:T(8,128)S(1)} %get-tuple-element.18), kind=kOutput, calls=%fused_computation.26 | convolution fusion | flops 687800320 | bytes 22999040 | tf_op jit(solution)/shard_map/fhqk,fkhd->fhqd/dot_general | solution.py:125
  105.2 0.0 copy-start.11
  105.2 0.9 fusion.40
  106.1 0.3 multiply_reduce_fusion.2
  106.4 0.2 fusion.27
  106.6 2.1 %copy.73 = bf16[1,512,640]{2,0,1:T(2,128)(2,1)} copy(bf16[1,512,640]{2,1,0:T(8,128)(2,1)S(1)} %fusion.27) | data formatting | bytes 1310720 | tf_op jit(solution)/shard_map/convert_element_type | solution.py:36
  108.7 0.5 broadcast.133
  109.3 5.6 %reduce.17 = bf16[512,640]{1,0:T(8,128)(2,1)S(1)} reduce(bf16[512,1,640]{2,1,0:T(2,128)(2,1)} %bitcast.64, bf16[]{:T(256)} %broadcast.133), dimensions={1}, to_apply=%bitcast.61.reduce_sub_computation | reduce | bytes 1310722
  114.8 0.2 reshape.213
  115.0 23.7 %all_to_all.8 = bf16[8,2,20480]{2,1,0:T(2,128)(2,1)S(1)} all-to-all(bf16[8,2,20480]{2,1,0:T(2,128)(2,1)S(1)} %reshape.213), channel_id=1, replica_groups=mesh['groups'=2,'frame'=8,'row'=2] {'frame'}, dimensions={0} | all-to-all | bytes 1310720 | tf_op jit(solution)/shard_map/all_to_all | solution.py:133
  138.7 0.6 reshape.214
  139.4 3.4 %convolution_convert_fusion = bf16[512,1920]{1,0:T(8,128)(2,1)S(1)} fusion(bf16[640,1920]{1,0:T(8,128)(2,1)} %param.16, bf16[1,512,640]{2,0,1:T(2,128)(2,1)S(1)} %bitcast.76), kind=kOutput, calls=%fused_computation.6 | convolution fusion | flops 1259274240 | bytes 5079040 | tf_op jit(solution)/shard_map/dot_general | solution.py:42
  142.8 1.1 fusion.36
  143.9 1.6 copy.66
  145.6 1.7 copy.57
  147.3 0.8 copy.67
  148.0 1.6 copy.58
  149.6 0.8 copy.65
  150.4 1.7 copy.59
  152.1 2.8 %multiply_reduce_fusion.1 = (f32[64,10,8]{2,1,0:T(8,128)S(1)}, f32[64,10,8,8]{2,3,1,0:T(8,128)S(1)}) fusion(bf16[8,64,10,64]{3,0,2,1:T(8,128)(2,1)} %copy.57, bf16[8,64,10,64]{3,0,2,1:T(8,128)(2,1)} %copy.58), kind=kOutput, calls=%fused_computation.12 | convolution fusion | flops 5319680 | bytes 1495040 | tf_op jit(solution)/shard_map/qphd,kphd->phqk/dot_general | solution.py:59
  154.9 1.2 fusion.6
  156.1 0.1 copy-done.8
  156.3 2.5 %fusion.5 = bf16[8,64,10,64]{3,0,2,1:T(8,128)(2,1)} fusion(bf16[8,64,10,64]{3,0,2,1:T(8,128)(2,1)S(1)} %copy-done.8, f32[64,10,8,8]{2,3,1,0:T(8,128)S(1)} %get-tuple-element.29, f32[8,64,10]{0,2,1:T(8,128)S(1)} %bitcast.78, f32[64,10,8]{2,1,0:T(8,128)S(1)} %get-tuple-element.28), kind=kOutput, calls=%fused_computation.10 | convolution fusion | flops 6021120 | bytes 1515520 | tf_op jit(solution)/shard_map/phqk,kphd->qphd/dot_general | solution.py:65
  158.8 2.0 %copy.61 = bf16[8,64,10,64]{1,3,2,0:T(8,128)(2,1)S(1)} copy(bf16[8,64,10,64]{3,0,2,1:T(8,128)(2,1)} %fusion.5) | data formatting | bytes 1310720 | tf_op jit(solution)/shard_map/convert_element_type | solution.py:67
  160.8 0.0 copy-start.10
  160.8 0.6 copy.62
  161.4 20.6 %all_to_all.9 = bf16[8,64,640]{2,1,0:T(8,128)(2,1)S(1)} all-to-all(bf16[8,64,640]{2,1,0:T(8,128)(2,1)S(1)} %copy.62), channel_id=1, replica_groups=mesh['groups'=2,'frame'=8,'row'=2] {'frame'}, dimensions={0} | all-to-all | bytes 1310720 | tf_op jit(solution)/shard_map/all_to_all | solution.py:136
  182.0 3.3 %convolution_add_fusion = f32[512,640]{1,0:T(8,128)} fusion(f32[512,640]{1,0:T(8,128)} %copy-done.3, bf16[512,640]{1,0:T(8,128)(2,1)S(1)} %bitcast.70, bf16[640,640]{1,0:T(8,128)(2,1)S(1)} %copy-done.10), kind=kOutput, calls=%fused_computation.16 | convolution fusion | flops 419758080 | bytes 4096000 | tf_op jit(solution)/shard_map/dot_general | solution.py:72
  (27 shorter events, 0.1 us)
Async XLA Ops:
  6.5 65.3 %copy-start = (bf16[640,1920]{1,0:T(8,128)(2,1)S(1)}, bf16[640,1920]{1,0:T(8,128)(2,1)}, u32[]{:S(2)}) copy-start(bf16[640,1920]{1,0:T(8,128)(2,1)} %param.13) | copy-start | bytes 7372804
  6.5 75.3 %all-gather.3.cloned.1.call-start = ((), (), s32[]{:S(2)}) async-start(), calls=%async_computation.2 | async-start | bytes 1966080 | tf_op jit(solution)/shard_map/all_gather | solution.py:112
  6.5 58.0 %collective-permute-start = (bf16[1,8,64,640]{3,2,1,0:T(8,128)(2,1)}, bf16[1,8,64,640]{3,2,1,0:T(8,128)(2,1)S(1)}, u32[]{:S(2)}, u32[]{:S(2)}) collective-permute-start(bf16[1,8,64,640]{3,2,1,0:T(8,128)(2,1)} %param.9), channel_id=1, source_target_pairs={{0,2},{2,4},{4,6},{6,8},{8,10},{10,12},{12,14},{1,3},{3,5},{5,7},{... | collective-permute-start | bytes 1966088 | tf_op jit(solution)/shard_map/ppermute | solution.py:16
  11.6 52.9 %collective-permute-start.1 = (bf16[1,8,64,640]{3,2,1,0:T(8,128)(2,1)}, bf16[1,8,64,640]{3,2,1,0:T(8,128)(2,1)}, u32[]{:S(2)}, u32[]{:S(2)}) collective-permute-start(bf16[1,8,64,640]{3,2,1,0:T(8,128)(2,1)} %param.9), channel_id=1, source_target_pairs={{2,0},{4,2},{6,4},{8,6},{10,8},{12,10},{14,12},{3,1},{5,3},{7,5},{... | collective-permute-start | bytes 1966088 | tf_op jit(solution)/shard_map/ppermute | solution.py:19
  67.0 1.7 copy-start.7
  69.5 1.1 copy-start.6
  70.6 1.3 copy-start.12
  71.5 2.2 %copy-start.4 = (f32[512,640]{1,0:T(8,128)}, f32[512,640]{1,0:T(8,128)S(1)}, u32[]{:S(2)}) copy-start(f32[512,640]{1,0:T(8,128)S(1)} %get-tuple-element.23) | copy-start | bytes 3932164
  75.0 19.1 %all-gather.5.cloned.1.call-start = ((), (), s32[]{:S(2)}) async-start(), calls=%async_computation.3 | async-start | bytes 1966080 | tf_op jit(solution)/shard_map/all_gather | solution.py:113
  86.5 7.6 %copy-start.2 = (f32[10,512,1024]{2,1,0:T(8,128)}, f32[10,512,1024]{2,1,0:T(8,128)S(1)}, u32[]{:S(2)}) copy-start(f32[10,512,1024]{2,1,0:T(8,128)S(1)} %get-tuple-element.25) | copy-start | bytes 62914564
  95.7 9.4 %copy-start.5 = (f32[512,640]{1,0:T(8,128)S(1)}, f32[512,640]{1,0:T(8,128)}, u32[]{:S(2)}) copy-start(f32[512,640]{1,0:T(8,128)} %copy-done.4) | copy-start | bytes 3932164
  95.8 9.4 %copy-start.9 = (bf16[640,640]{1,0:T(8,128)(2,1)S(1)}, bf16[640,640]{1,0:T(8,128)(2,1)}, u32[]{:S(2)}) copy-start(bf16[640,640]{1,0:T(8,128)(2,1)} %param.14) | copy-start | bytes 2457604
  105.2 1.2 copy-start.11
  106.1 2.6 %copy-start.3 = (f32[512,640]{1,0:T(8,128)}, f32[512,640]{1,0:T(8,128)S(1)}, u32[]{:S(2)}) copy-start(f32[512,640]{1,0:T(8,128)S(1)} %get-tuple-element.27) | copy-start | bytes 3932164
  154.9 1.3 copy-start.8
  160.8 21.2 %copy-start.10 = (bf16[640,640]{1,0:T(8,128)(2,1)S(1)}, bf16[640,640]{1,0:T(8,128)(2,1)}, u32[]{:S(2)}) copy-start(bf16[640,640]{1,0:T(8,128)(2,1)} %param.17) | copy-start | bytes 2457604
  182.0 3.3 %copy-start.1 = (bf16[640,1920]{1,0:T(8,128)(2,1)S(1)}, bf16[640,1920]{1,0:T(8,128)(2,1)}, u32[]{:S(2)}) copy-start(bf16[640,1920]{1,0:T(8,128)(2,1)} %param.13) | copy-start | bytes 7372804
Sparse Core Ops, SparseCore 0:
  75.1 6.6 all-gather.2
  83.4 10.5 all-gather.4
where the time goes:
time: 193 us; the launch traced here: 192 us
  blocking collectives  93.8 us (49%)
  matrix products  29.7 us (15%)
  local copies, waits for them, and re-layouts  25.7 us (13%)
  other arithmetic  16.2 us (8%)
  between operations  13.8 us (7%)
  starting transfers between devices  6.55 us (3%)
  waiting for transfers between devices  6.39 us (3%)
    psum x1, blocking collectives, body(): first, second = lax.psum((first, second), ('frame', 'row'))  49.5 us
    all_to_all x1, blocking collectives, body(): lax.all_to_all(normed, 'frame', split_axis=1, concat_axis=0, tiled=True)  23.7 us
    all_to_all x1, blocking collectives, body(): lax.all_to_all(result, 'frame', split_axis=0, concat_axis=1, tiled=True)  20.6 us
    unnamed x32, local copies, waits for them, and re-layouts  9.47 us
    dot_general x1, matrix products, body(): jnp.einsum('fhqk,fkhd->fhqd', weights, value_heads, preferred_element_typ...  9.35 us
    all_gather x1, waiting for transfers between devices, body(): key_piece = lax.all_gather(key_rows, 'row', axis=1, tiled=True)  6.1 us
    unnamed x1, other arithmetic  5.57 us
    dot_general x2, matrix products, project_three(): jnp.dot(inputs.reshape(-1, channels), weight, preferred_element_type=jnp....  5.31 us
  transfers between devices with their start and end apart: 4, of which 1 were waited for; matrix products, arithmetic and copies ran while one was open for 6% of the time, Pallas kernels for 0%

commit v1 on v0

--- a/solution.py
+++ b/solution.py
@@ -6,6 +6,17 @@
 HEADS = 10
 GROUPS = 32
 epsilon = 1e-05
+
+
+def split_up(x, dim, length):
+    before, after = (x.shape[:dim], x.shape[dim + 1 :])
+    return jnp.moveaxis(x.reshape(*before, length, -1, *after), dim, 0)
+
+
+def joined_along(blocks, dim):
+    shape = list(blocks.shape[1:])
+    shape[dim] *= blocks.shape[0]
+    return jnp.moveaxis(blocks, 0, dim).reshape(shape)
 
 
 def padded_2(block, sides, width):
@@ -130,7 +141,14 @@
     attended = jnp.transpose(attended, (0, 2, 1, 3)).reshape(frames, pixels, channels)
     spaced = add_projected(stepped, attended, space_out)
     normed = layer_norm(spaced, time_norm)
-    moved = lax.all_to_all(normed, "frame", split_axis=1, concat_axis=0, tiled=True)
+    size, place_2 = (lax.axis_size("frame"), lax.axis_index("frame"))
+    blocks = split_up(normed, 1, size)
+    outs = [blocks[place_2]]
+    for step in range(1, size):
+        sent = blocks[place_2 ^ step]
+        outs.append(lax.ppermute(sent, "frame", [(i_2, i_2 ^ step) for i_2 in range(size)]))
+    blocks = jnp.stack(outs)[place_2 ^ jnp.arange(size)]
+    moved = joined_along(blocks, 0)
     queries, key_rows, values = project_three(moved, time_qkv)
     result = time_attend(queries, key_rows, values)
     result = lax.all_to_all(result, "frame", split_axis=0, concat_axis=1, tiled=True)

time: 193 us -> 183 us (0.948)
  blocking collectives: 93.8 us -> 72.7 us
  starting transfers between devices: 6.55 us -> 17.6 us
  waiting for transfers between devices: 6.39 us -> 14.7 us
  other arithmetic: 16.2 us -> 10.7 us
  local copies, waits for them, and re-layouts: 25.7 us -> 23.6 us
    all_to_all x1 -> x0, blocking collectives: 23.7 us -> none  [body(): lax.all_to_all(normed, 'frame', split_axis=1, concat_axis=0, tiled=True)]
    ppermute x0 -> x7, starting transfers between devices: none -> 11.2 us  [body(): lax.ppermute(sent, 'frame', [(i_2, i_2 ^ step) for i_2 in range(size)])]
    ppermute x0 -> x7, waiting for transfers between devices: none -> 8.22 us  [body(): lax.ppermute(sent, 'frame', [(i_2, i_2 ^ step) for i_2 in range(size)])]
    unnamed x1 -> x0, other arithmetic: 5.57 us -> none
    all_to_all x1, blocking collectives: 20.6 us -> 23.2 us  [body(): lax.all_to_all(result, 'frame', split_axis=0, concat_axis=1, tiled=True)]
    convert_element_type x1 -> x0, local copies, waits for them, and re-layouts: 2.07 us -> none  [layer_norm(): return (shifted * lax.rsqrt(spread + epsilon) * gain).astype(jnp.bfloat16)]
    unnamed x32 -> x35, local copies, waits for them, and re-layouts: 9.47 us -> 8.62 us
  transfers between devices with their start and end apart: 4 -> 11, of which waited for: 1 -> 2; matrix products, arithmetic and copies ran while one was open for 6% -> 6% of each run, Pallas kernels for 0% -> 0%
where the time goes in v1:
time: 183 us
  blocking collectives  72.7 us (40%)
  matrix products  29.4 us (16%)
  local copies, waits for them, and re-layouts  23.6 us (13%)
  starting transfers between devices  17.6 us (10%)
  waiting for transfers between devices  14.7 us (8%)
  between operations  13.9 us (8%)
  other arithmetic  10.7 us (6%)
    psum x1, blocking collectives, body(): first, second = lax.psum((first, second), ('frame', 'row'))  49.5 us
    all_to_all x1, blocking collectives, body(): lax.all_to_all(result, 'frame', split_axis=0, concat_axis=1, tiled=True)  23.2 us
    ppermute x7, starting transfers between devices, body(): lax.ppermute(sent, 'frame', [(i_2, i_2 ^ step) for i_2 in range(size)])  11.2 us
    dot_general x1, matrix products, body(): jnp.einsum('fhqk,fkhd->fhqd', weights, value_heads, preferred_element_typ...  9.13 us
    unnamed x35, local copies, waits for them, and re-layouts  8.62 us
    ppermute x7, waiting for transfers between devices, body(): lax.ppermute(sent, 'frame', [(i_2, i_2 ^ step) for i_2 in range(size)])  8.22 us
    all_gather x1, waiting for transfers between devices, body(): key_piece = lax.all_gather(key_rows, 'row', axis=1, tiled=True)  6.1 us
    dot_general x2, matrix products, project_three(): jnp.dot(inputs.reshape(-1, channels), weight, preferred_element_type=jnp....  5.31 us
  transfers between devices with their start and end apart: 11, of which 2 were waited for; matrix products, arithmetic and copies ran while one was open for 6% of the time, Pallas kernels for 0%

profile of v1, /device:TPU:0, one launch (start us, length us, event | category | flops | bytes accessed | tf_op | source)
XLA Modules:
  0.0 182.6 jit_solution(16572023374346034298)
XLA Ops:
  6.5 5.0 %collective-permute-start = (bf16[1,8,64,640]{3,2,1,0:T(8,128)(2,1)}, bf16[1,8,64,640]{3,2,1,0:T(8,128)(2,1)S(1)}, u32[]{:S(2)}, u32[]{:S(2)}) collective-permute-start(bf16[1,8,64,640]{3,2,1,0:T(8,128)(2,1)} %param.9), channel_id=1, source_target_pairs={{0,2},{2,4},{4,6},{6,8},{8,10},{10,12},{12,14},{1,3},{3,5},{5,7},{... | collective-permute-start | bytes 1966088 | tf_op jit(solution)/shard_map/ppermute | solution.py:27
  11.6 1.3 collective-permute-start.1
  12.9 1.3 convert_reduce_fusion
  14.2 0.1 reduce_sum.87
  14.3 0.1 reduce_sum.90
  14.4 0.1 reduce_sum.88
  14.5 0.1 reduce_sum.91
  14.6 49.5 %all-reduce = (f32[32]{0:T(128)S(1)}, f32[32]{0:T(128)S(1)}) all-reduce(f32[32]{0:T(128)S(1)} %reduce_sum.91, f32[32]{0:T(128)S(1)} %reduce_sum.88), channel_id=1, replica_groups=mesh['groups'=2,'frame'=8,'row'=2] {'frame','row'}, use_global_device_ids=true, to_apply=%region_5.6 | all-reduce | flops 64 | bytes 512 | tf_op jit(solution)/shard_map/psum | solution.py:99
  64.1 0.1 mul.98
  64.2 0.1 mul.99
  64.3 0.1 sub.68
  64.4 0.1 sub.69
  64.5 2.5 %fusion.8 = bf16[3,8,64,640]{3,2,1,0:T(8,128)(2,1)S(1)} fusion(bf16[1,8,64,640]{3,2,1,0:T(8,128)(2,1)} %collective-permute-done.1, bf16[1,8,64,640]{3,2,1,0:T(8,128)(2,1)} %param.9, bf16[1,8,64,640]{3,2,1,0:T(8,128)(2,1)S(1)} %collective-permute-done, f32[640]{0:T(1024)} %param.10, f32[640]{0:T(1024)S(1)} %mul.99, f32[640]{0:T(1024)S(1)} %sub.69, ...), kind=kLoop, calls=%fused_computation.16 | loop fusion | flops 11796480 | bytes 3939843 | tf_op jit(solution)/shard_map/jit(_where)/select_n | solution.py:110
  67.1 0.2 fusion.36
  67.3 1.5 copy-done.7
  68.7 0.8 fusion.19
  69.5 0.7 fusion.21
  70.3 0.3 copy-done.6
  70.6 0.9 fusion.37
  71.6 0.3 multiply_reduce_fusion.3
  71.9 1.9 %fusion.4 = bf16[1,512,1920]{2,1,0:T(8,128)(2,1)S(1)} fusion(bf16[640,1920]{1,0:T(8,128)(2,1)S(1)} %copy-done, f32[512,640]{1,0:T(8,128)S(1)} %get-tuple-element.31, f32[640]{0:T(1024)S(1)} %copy-done.12, f32[512]{0:T(512)S(1)} %add_rsqrt_fusion.1, f32[512]{0:T(512)S(1)} %broadcast_multiply_fusion.1), kind=kOutput, calls=%fused_computation.9 | convolution fusion | flops 1260584960 | bytes 5741056 | tf_op jit(solution)/shard_map/dot_general | solution.py:53
  73.8 1.2 fusion.35
  75.0 0.0 all-gather.3.cloned.1.call-update
  75.0 0.0 all-gather.5.cloned.1.call-start
  75.1 0.3 copy.37
  75.4 0.4 all-gather.5.cloned.1.call-update
  75.8 6.1 %all-gather.3.cloned.1.call-done = bf16[1,1024,640]{2,1,0:T(8,128)(2,1)} async-done(((bf16[1,512,640]{2,1,0:T(8,128)(2,1)}), bf16[1,1024,640]{2,1,0:T(8,128)(2,1)}) %all-gather.3.cloned.1.call-update) | async-done | bytes 1310736 | tf_op jit(solution)/shard_map/all_gather | solution.py:123
  81.9 1.6 copy.38
  83.5 3.0 %multiply_reduce_fusion = (f32[10,512]{1,0:T(8,128)S(1)}, f32[10,512,1024]{2,1,0:T(8,128)S(1)}) fusion(bf16[512,10,64]{0,2,1:T(8,128)(2,1)S(1)} %bitcast.93, bf16[1024,10,64]{0,2,1:T(8,128)(2,1)S(1)} %bitcast.88), kind=kOutput, calls=%fused_computation.2 | convolution fusion | flops 681569280 | bytes 22958080 | tf_op jit(solution)/shard_map/fqhd,fkhd->fhqk/dot_general | solution.py:128
  86.5 4.6 %fusion = f32[10,512]{1,0:T(8,128)S(1)} fusion(f32[10,512,1024]{2,1,0:T(8,128)S(1)} %get-tuple-element.33, f32[10,512]{1,0:T(8,128)S(1)} %get-tuple-element.32), kind=kLoop, calls=%fused_computation.3 | loop fusion | flops 15723520 | bytes 21012480 | tf_op jit(solution)/shard_map/reduce_sum | solution.py:134
  91.1 3.0 %copy-done.2 = f32[10,512,1024]{2,1,0:T(8,128)} copy-done((f32[10,512,1024]{2,1,0:T(8,128)}, f32[10,512,1024]{2,1,0:T(8,128)S(1)}, u32[]{:S(2)}) %copy-start.2) | copy-done | bytes 20971544
  94.1 0.0 all-gather.5.cloned.1.call-done
  94.1 1.6 copy.39
  95.8 9.1 %divide_convert_fusion = bf16[10,512,64]{1,2,0:T(8,128)(2,1)S(1)} fusion(bf16[1024,10,64]{0,2,1:T(8,128)(2,1)S(1)} %bitcast.100, f32[10,512,1024]{2,1,0:T(8,128)} %copy-done.2, f32[10,512]{1,0:T(8,128)S(1)} %get-tuple-element.32, f32[10,512]{1,0:T(8,128)S(1)} %get-tuple-element.27, f32[10,512]{1,0:T(8,128)S(1)} %get-tuple-element.26), kind=kOutput, calls=%fused_computation.27 | convolution fusion | flops 687800320 | bytes 22999040 | tf_op jit(solution)/shard_map/fhqk,fkhd->fhqd/dot_general | solution.py:136
  105.0 0.9 fusion.38
  105.9 0.3 multiply_reduce_fusion.2
  106.2 0.2 multiply_convert_fusion.1
  106.4 0.1 dynamic-slice_bitcast_fusion
  106.5 0.4 copy-done.3
  106.9 1.7 collective-permute-start.2
  108.7 1.5 collective-permute-start.3
  110.2 0.3 collective-permute-start.4
  110.4 2.7 %collective-permute-start.5 = (bf16[1,64,640]{2,1,0:T(8,128)(2,1)S(1)}, bf16[1,64,640]{2,1,0:T(8,128)(2,1)S(1)}, u32[]{:S(2)}, u32[]{:S(2)}) collective-permute-start(bf16[1,64,640]{2,1,0:T(8,128)(2,1)S(1)} %get-tuple-element.21), channel_id=1, source_target_pairs={{0,8},{2,10},{4,12},{6,14},{8,0},{10,2},{12,4},{14,6},{1,9},{3,11}... | collective-permute-start | bytes 245768 | tf_op jit(solution)/shard_map/ppermute | solution.py:149
  113.1 1.4 collective-permute-start.6
  114.5 3.3 %collective-permute-start.7 = (bf16[1,64,640]{2,1,0:T(8,128)(2,1)S(1)}, bf16[1,64,640]{2,1,0:T(8,128)(2,1)S(1)}, u32[]{:S(2)}, u32[]{:S(2)}) collective-permute-start(bf16[1,64,640]{2,1,0:T(8,128)(2,1)S(1)} %get-tuple-element.19), channel_id=1, source_target_pairs={{0,12},{2,14},{4,8},{6,10},{8,4},{10,6},{12,0},{14,2},{1,13},{3,15... | collective-permute-start | bytes 245768 | tf_op jit(solution)/shard_map/ppermute | solution.py:149
  117.9 0.3 collective-permute-start.8
  118.2 8.2 %collective-permute-done.6 = bf16[1,64,640]{2,1,0:T(8,128)(2,1)S(1)} collective-permute-done((bf16[1,64,640]{2,1,0:T(8,128)(2,1)S(1)}, bf16[1,64,640]{2,1,0:T(8,128)(2,1)S(1)}, u32[]{:S(2)}, u32[]{:S(2)}) %collective-permute-start.6) | collective-permute-done | bytes 81952 | tf_op jit(solution)/shard_map/ppermute | solution.py:149
  126.5 0.7 gather_fusion
  127.2 3.4 %convolution_convert_fusion = bf16[512,1920]{1,0:T(8,128)(2,1)S(1)} fusion(bf16[512,640]{1,0:T(8,128)(2,1)S(1)} %bitcast.103, bf16[640,1920]{1,0:T(8,128)(2,1)} %param.16), kind=kOutput, calls=%fused_computation.7 | convolution fusion | flops 1259274240 | bytes 5079040 | tf_op jit(solution)/shard_map/dot_general | solution.py:53
  130.6 1.1 fusion.34
  131.8 1.6 copy.51
  133.4 1.7 copy.43
  135.1 0.8 copy.52
  135.9 1.6 copy.44
  137.5 0.8 copy.50
  138.2 1.7 copy.45
  139.9 2.8 %multiply_reduce_fusion.1 = (f32[64,10,8]{2,1,0:T(8,128)S(1)}, f32[64,10,8,8]{2,3,1,0:T(8,128)S(1)}) fusion(bf16[8,64,10,64]{3,0,2,1:T(8,128)(2,1)} %copy.43, bf16[8,64,10,64]{3,0,2,1:T(8,128)(2,1)} %copy.44), kind=kOutput, calls=%fused_computation.13 | convolution fusion | flops 5319680 | bytes 1495040 | tf_op jit(solution)/shard_map/qphd,kphd->phqk/dot_general | solution.py:70
  142.8 1.2 fusion.6
  144.0 0.1 copy-done.8
  144.1 2.5 %fusion.5 = bf16[8,64,10,64]{3,0,2,1:T(8,128)(2,1)} fusion(bf16[8,64,10,64]{3,0,2,1:T(8,128)(2,1)S(1)} %copy-done.8, f32[64,10,8,8]{2,3,1,0:T(8,128)S(1)} %get-tuple-element.37, f32[8,64,10]{0,2,1:T(8,128)S(1)} %bitcast.104, f32[64,10,8]{2,1,0:T(8,128)S(1)} %get-tuple-element.36), kind=kOutput, calls=%fused_computation.11 | convolution fusion | flops 6021120 | bytes 1515520 | tf_op jit(solution)/shard_map/phqk,kphd->qphd/dot_general | solution.py:76
  146.6 2.0 %copy.47 = bf16[8,64,10,64]{1,3,2,0:T(8,128)(2,1)S(1)} copy(bf16[8,64,10,64]{3,0,2,1:T(8,128)(2,1)} %fusion.5) | data formatting | bytes 1310720 | tf_op jit(solution)/shard_map/convert_element_type | solution.py:78
  148.6 0.6 copy.48
  149.3 23.2 %all_to_all.4 = bf16[8,64,640]{2,1,0:T(8,128)(2,1)S(1)} all-to-all(bf16[8,64,640]{2,1,0:T(8,128)(2,1)S(1)} %copy.48), channel_id=1, replica_groups=mesh['groups'=2,'frame'=8,'row'=2] {'frame'}, dimensions={0} | all-to-all | bytes 1310720 | tf_op jit(solution)/shard_map/all_to_all | solution.py:154
  172.5 3.3 %convolution_add_fusion = f32[512,640]{1,0:T(8,128)} fusion(f32[512,640]{1,0:T(8,128)} %copy-done.3, bf16[512,640]{1,0:T(8,128)(2,1)S(1)} %bitcast.94, bf16[640,640]{1,0:T(8,128)(2,1)S(1)} %copy-done.10), kind=kOutput, calls=%fused_computation.17 | convolution fusion | flops 419758080 | bytes 4096000 | tf_op jit(solution)/shard_map/dot_general | solution.py:83
  (46 shorter events, 0.2 us)
Async XLA Ops:
  6.5 65.3 %copy-start = (bf16[640,1920]{1,0:T(8,128)(2,1)S(1)}, bf16[640,1920]{1,0:T(8,128)(2,1)}, u32[]{:S(2)}) copy-start(bf16[640,1920]{1,0:T(8,128)(2,1)} %param.13) | copy-start | bytes 7372804
  6.5 75.3 %all-gather.3.cloned.1.call-start = ((), (), s32[]{:S(2)}) async-start(), calls=%async_computation.1 | async-start | bytes 1966080 | tf_op jit(solution)/shard_map/all_gather | solution.py:123
  6.5 58.0 %collective-permute-start = (bf16[1,8,64,640]{3,2,1,0:T(8,128)(2,1)}, bf16[1,8,64,640]{3,2,1,0:T(8,128)(2,1)S(1)}, u32[]{:S(2)}, u32[]{:S(2)}) collective-permute-start(bf16[1,8,64,640]{3,2,1,0:T(8,128)(2,1)} %param.9), channel_id=1, source_target_pairs={{0,2},{2,4},{4,6},{6,8},{8,10},{10,12},{12,14},{1,3},{3,5},{5,7},{... | collective-permute-start | bytes 1966088 | tf_op jit(solution)/shard_map/ppermute | solution.py:27
  11.6 52.9 %collective-permute-start.1 = (bf16[1,8,64,640]{3,2,1,0:T(8,128)(2,1)}, bf16[1,8,64,640]{3,2,1,0:T(8,128)(2,1)}, u32[]{:S(2)}, u32[]{:S(2)}) collective-permute-start(bf16[1,8,64,640]{3,2,1,0:T(8,128)(2,1)} %param.9), channel_id=1, source_target_pairs={{2,0},{4,2},{6,4},{8,6},{10,8},{12,10},{14,12},{3,1},{5,3},{7,5},{... | collective-permute-start | bytes 1966088 | tf_op jit(solution)/shard_map/ppermute | solution.py:30
  67.0 1.7 copy-start.7
  69.5 1.1 copy-start.6
  70.6 1.3 copy-start.12
  71.5 2.2 %copy-start.4 = (f32[512,640]{1,0:T(8,128)}, f32[512,640]{1,0:T(8,128)S(1)}, u32[]{:S(2)}) copy-start(f32[512,640]{1,0:T(8,128)S(1)} %get-tuple-element.31) | copy-start | bytes 3932164
  75.0 19.1 %all-gather.5.cloned.1.call-start = ((), (), s32[]{:S(2)}) async-start(), calls=%async_computation.2 | async-start | bytes 1966080 | tf_op jit(solution)/shard_map/all_gather | solution.py:124
  86.5 7.6 %copy-start.2 = (f32[10,512,1024]{2,1,0:T(8,128)}, f32[10,512,1024]{2,1,0:T(8,128)S(1)}, u32[]{:S(2)}) copy-start(f32[10,512,1024]{2,1,0:T(8,128)S(1)} %get-tuple-element.33) | copy-start | bytes 62914564
  95.8 9.2 %copy-start.5 = (f32[512,640]{1,0:T(8,128)S(1)}, f32[512,640]{1,0:T(8,128)}, u32[]{:S(2)}) copy-start(f32[512,640]{1,0:T(8,128)} %copy-done.4) | copy-start | bytes 3932164
  95.8 9.2 %copy-start.9 = (bf16[640,640]{1,0:T(8,128)(2,1)S(1)}, bf16[640,640]{1,0:T(8,128)(2,1)}, u32[]{:S(2)}) copy-start(bf16[640,640]{1,0:T(8,128)(2,1)} %param.14) | copy-start | bytes 2457604
  104.9 1.2 copy-start.11
  105.9 1.1 copy-start.3
  106.9 7.6 %collective-permute-start.2 = (bf16[1,64,640]{2,1,0:T(8,128)(2,1)S(1)}, bf16[1,64,640]{2,1,0:T(8,128)(2,1)S(1)}, u32[]{:S(2)}, u32[]{:S(2)}) collective-permute-start(bf16[1,64,640]{2,1,0:T(8,128)(2,1)S(1)} %get-tuple-element.24), channel_id=1, source_target_pairs={{0,2},{2,0},{4,6},{6,4},{8,10},{10,8},{12,14},{14,12},{1,3},{3,1},... | collective-permute-start | bytes 245768 | tf_op jit(solution)/shard_map/ppermute | solution.py:149
  108.7 9.2 %collective-permute-start.3 = (bf16[1,64,640]{2,1,0:T(8,128)(2,1)S(1)}, bf16[1,64,640]{2,1,0:T(8,128)(2,1)S(1)}, u32[]{:S(2)}, u32[]{:S(2)}) collective-permute-start(bf16[1,64,640]{2,1,0:T(8,128)(2,1)S(1)} %get-tuple-element.23), channel_id=1, source_target_pairs={{0,4},{2,6},{4,0},{6,2},{8,12},{10,14},{12,8},{14,10},{1,5},{3,7},... | collective-permute-start | bytes 245768 | tf_op jit(solution)/shard_map/ppermute | solution.py:149
  110.2 8.0 %collective-permute-start.4 = (bf16[1,64,640]{2,1,0:T(8,128)(2,1)S(1)}, bf16[1,64,640]{2,1,0:T(8,128)(2,1)S(1)}, u32[]{:S(2)}, u32[]{:S(2)}) collective-permute-start(bf16[1,64,640]{2,1,0:T(8,128)(2,1)S(1)} %get-tuple-element.22), channel_id=1, source_target_pairs={{0,6},{2,4},{4,2},{6,0},{8,14},{10,12},{12,10},{14,8},{1,7},{3,5},... | collective-permute-start | bytes 245768 | tf_op jit(solution)/shard_map/ppermute | solution.py:149
  110.4 7.8 %collective-permute-start.5 = (bf16[1,64,640]{2,1,0:T(8,128)(2,1)S(1)}, bf16[1,64,640]{2,1,0:T(8,128)(2,1)S(1)}, u32[]{:S(2)}, u32[]{:S(2)}) collective-permute-start(bf16[1,64,640]{2,1,0:T(8,128)(2,1)S(1)} %get-tuple-element.21), channel_id=1, source_target_pairs={{0,8},{2,10},{4,12},{6,14},{8,0},{10,2},{12,4},{14,6},{1,9},{3,11}... | collective-permute-start | bytes 245768 | tf_op jit(solution)/shard_map/ppermute | solution.py:149
  113.1 13.3 %collective-permute-start.6 = (bf16[1,64,640]{2,1,0:T(8,128)(2,1)S(1)}, bf16[1,64,640]{2,1,0:T(8,128)(2,1)S(1)}, u32[]{:S(2)}, u32[]{:S(2)}) collective-permute-start(bf16[1,64,640]{2,1,0:T(8,128)(2,1)S(1)} %get-tuple-element.20), channel_id=1, source_target_pairs={{0,10},{2,8},{4,14},{6,12},{8,2},{10,0},{12,6},{14,4},{1,11},{3,9}... | collective-permute-start | bytes 245768 | tf_op jit(solution)/shard_map/ppermute | solution.py:149
  114.5 11.9 %collective-permute-start.7 = (bf16[1,64,640]{2,1,0:T(8,128)(2,1)S(1)}, bf16[1,64,640]{2,1,0:T(8,128)(2,1)S(1)}, u32[]{:S(2)}, u32[]{:S(2)}) collective-permute-start(bf16[1,64,640]{2,1,0:T(8,128)(2,1)S(1)} %get-tuple-element.19), channel_id=1, source_target_pairs={{0,12},{2,14},{4,8},{6,10},{8,4},{10,6},{12,0},{14,2},{1,13},{3,15... | collective-permute-start | bytes 245768 | tf_op jit(solution)/shard_map/ppermute | solution.py:149
  117.9 8.6 %collective-permute-start.8 = (bf16[1,64,640]{2,1,0:T(8,128)(2,1)S(1)}, bf16[1,64,640]{2,1,0:T(8,128)(2,1)S(1)}, u32[]{:S(2)}, u32[]{:S(2)}) collective-permute-start(bf16[1,64,640]{2,1,0:T(8,128)(2,1)S(1)} %get-tuple-element.18), channel_id=1, source_target_pairs={{0,14},{2,12},{4,10},{6,8},{8,6},{10,4},{12,2},{14,0},{1,15},{3,13... | collective-permute-start | bytes 245768 | tf_op jit(solution)/shard_map/ppermute | solution.py:149
  142.8 1.3 copy-start.8
  148.6 23.8 %copy-start.10 = (bf16[640,640]{1,0:T(8,128)(2,1)S(1)}, bf16[640,640]{1,0:T(8,128)(2,1)}, u32[]{:S(2)}) copy-start(bf16[640,640]{1,0:T(8,128)(2,1)} %param.17) | copy-start | bytes 2457604
  172.5 3.3 %copy-start.1 = (bf16[640,1920]{1,0:T(8,128)(2,1)S(1)}, bf16[640,1920]{1,0:T(8,128)(2,1)}, u32[]{:S(2)}) copy-start(bf16[640,1920]{1,0:T(8,128)(2,1)} %param.13) | copy-start | bytes 7372804
Sparse Core Ops, SparseCore 0:
  75.1 6.6 all-gather.2
  83.4 10.5 all-gather.4
